TPU v7x, 32 devices: a whole 2x2x4 slice. The times are simulated.
32 devices in a mesh: leaf: 2 (over x), rows: 16 (over z, y, core).
Axes of the slice: x: 2, y: 2, z: 4, core: 2. Of those that a mesh axis runs over, the one named last changes fastest.
Arguments:
- features: bfloat16 [262144, 256], P(('leaf', 'rows')), parts along dimension 0, may hold values from -80 to 80
- node_ids: int32 [262144], P(('leaf', 'rows')), parts along dimension 0, may hold values from -1 to 15, as said below
- labels: int32 [262144], P(('leaf', 'rows')), parts along dimension 0, may hold values from 0 to 15
- owners: int32 [32], P('leaf'), parts along dimension 0, may hold values from 0 to 15, each once
Outputs:
- hyperplanes: float32 [32, 16, 256], P(('leaf', 'rows')), parts along dimension 0
- scores: float32 [16, 262144], P(None, ('leaf', 'rows')), parts along dimension 1
There are 2 independent parts, one for each index of `leaf`. A program takes and returns all parts, laid end to end along the dimension named above; each array names one. Nothing has to cross between parts.
Inputs may be any that keep to these rules, and one draw needn't show every extreme that they name: `node_ids`: on rows device d, row p of node n's segment (local row n * 512 + p) holds n or -1; the live rows of a segment come first and there is at least one; some segment of every device is full. Each node number appears once in owners; node n is owned by the device of rows with index owners[n].
All inputs are finite; a program needn't handle non-finite values.
Results may differ from a plain program's by a relative error of at most 0.0035.
Values may be sent and summed in bfloat16 or wider, within the bound.
A program may use at most 128 MiB of HBM per device.

v0:
```python
import functools
import jax
import jax.numpy as jnp
from jax import lax
from jax.experimental import pallas as pl
from jax.experimental.pallas import tpu as pltpu
from jax.sharding import PartitionSpec as P

CLASSES = 16
LANES = 128
RIDGE = 0.1
HIGHEST = lax.Precision.HIGHEST
TN = (((0,), (0,)), ((), ()))
NT = (((1,), (1,)), ((), ()))


def iota(shape, dim):
    return lax.broadcasted_iota(jnp.int32, shape, dim)


def partner_of(me, bit):
    width = 1 << bit
    return me + width * (1 - 2 * ((me // width) % 2))


def one_partial(node, q, x_ref, ids_ref, labels_ref, out_ref):
    seg, feat = x_ref.shape[1:]
    half = feat // 2
    pieces = seg // LANES
    ids = ids_ref[pl.ds(node * pieces, pieces), :]
    tags = labels_ref[pl.ds(node * pieces, pieces), :]
    live = ids == node
    length = jnp.sum(live.astype(jnp.float32), axis=(0, 1), keepdims=True)
    x = x_ref[node]
    position = iota((seg, 1), 0).astype(jnp.float32)
    x = jnp.where(position < length, x, jnp.zeros((), x.dtype))
    tags = jnp.where(live, tags, -1)
    hot = jnp.concatenate(
        [tags[k : k + 1, :] == iota((CLASSES, LANES), 0) for k in range(pieces)], axis=1
    )
    hot = hot.astype(jnp.float32).astype(jnp.bfloat16)
    moment = lax.dot_general(x, x, TN, preferred_element_type=jnp.float32)
    sums = jnp.dot(hot, x, preferred_element_type=jnp.float32)
    counts = lax.dot_general(
        jnp.ones((8, seg), jnp.bfloat16), hot, NT, preferred_element_type=jnp.float32
    )
    row, col = iota((half, half), 0), iota((half, half), 1)
    low = moment[half:, half:]
    packed = jnp.where(row >= col, moment[:half, :half], low)
    diag = jnp.sum(jnp.where(row == col, low, 0.0), axis=0, keepdims=True)
    out_ref[q, 0:half, 0:half] = packed
    out_ref[q, 0:half, half:feat] = moment[:half, half:]
    out_ref[q, half : half + CLASSES, :] = sums
    top = half + CLASSES
    out_ref[q, top : top + 8, 0:half] = jnp.concatenate(
        [counts, jnp.zeros((8, half - CLASSES), jnp.float32)], axis=1
    )
    out_ref[q, top : top + 8, half:feat] = jnp.broadcast_to(diag, (8, half))


def reduce_kernel(
    n,
    owners_hbm,
    x_hbm,
    ids_hbm,
    labels_hbm,
    out_ref,
    owners_ref,
    x_ref,
    ids_ref,
    labels_ref,
    acc,
    landed,
    load_sems,
    send_sems,
    recv_sems,
):
    bits = n.bit_length() - 1
    me = lax.axis_index("rows")
    barrier = pltpu.get_barrier_semaphore()
    pairs = [(owners_hbm, owners_ref), (ids_hbm, ids_ref), (labels_hbm, labels_ref), (x_hbm, x_ref)]
    loads = [pltpu.make_async_copy(a, b, load_sems.at[k]) for k, (a, b) in enumerate(pairs)]
    for load in loads:
        load.start()
    for bit in range(bits):
        pl.semaphore_signal(barrier, inc=1, device_id={"rows": partner_of(me, bit)})
    for load in loads:
        load.wait()
    pl.semaphore_wait(barrier, bits)

    def copy_of(step, q):
        return pltpu.make_async_remote_copy(
            src_ref=acc.at[q],
            dst_ref=landed.at[q],
            send_sem=send_sems.at[q],
            recv_sem=recv_sems.at[q],
            device_id={"rows": partner_of(me, step)},
        )

    def partial(q):
        slot = 0
        for b in range(bits):
            mine, theirs = (me // (1 << b)) % 2, (q // (1 << (bits - 1 - b))) % 2
            slot = slot + (1 << b) * ((mine + theirs) % 2)
        node = 0
        for k in range(n):
            node = jnp.where(owners_ref[k] == slot, k, node)
        one_partial(node, q, x_ref, ids_ref, labels_ref, acc)

    def finish(step, q):
        half = n >> (step + 1)
        copy_of(step, q + half).wait_recv()
        acc[q] = acc[q] + landed[q + half]

    quarter = n // 4

    def turn(i):
        low = quarter - 1 - i % quarter
        for b in range(bits - 2):
            yield (low // (1 << b)) % 2, bits - 3 - b
        yield 1 - i // quarter, bits - 2

    def block_at(i):
        return sum(bit * (1 << place) for bit, place in turn(i))

    def pair(i, carry):
        q = block_at(i)
        partial(q + n // 2)
        copy_of(0, q + n // 2).start()
        partial(q)

        @pl.when(i >= 1)
        def _():
            before = block_at(i - 1)
            finish(0, before)

            @pl.when(i - 1 < quarter)
            def _():
                copy_of(1, before).start()

        @pl.when(i >= quarter + 2)
        def _():
            before = block_at(i - 2)
            finish(1, before)

            @pl.when(before >= n // 8)
            def _():
                copy_of(2, before).start()

        return carry

    lax.fori_loop(0, n // 2, pair, 0)
    finish(0, 0)
    ready = {(0, block_at(i)): i for i in range(n // 2)}
    for step in range(1, bits):
        half = n >> (step + 1)
        for q in range(half):
            ready[step, q] = max(ready[step - 1, q], ready[step - 1, q + half] + 1)
    late = {block_at(n // 2 - 2), block_at(n // 2 - 1)}
    rest = [(step, q) for step, q in ready if step > 1 or (step == 1 and q in late)]
    for step, q in sorted(rest, key=lambda event: (ready[event], event)):
        if step == bits - 1:
            copy_of(step, 1).wait_recv()
            out_ref[...] = acc[0] + landed[1]
        else:
            finish(step, q)
            if q >= n >> (step + 2):
                copy_of(step + 1, q).start()
    for step in range(bits):
        half = n >> (step + 1)
        for q in range(half, 2 * half):
            copy_of(step, q).wait_send()


def lane_of(x, lane):
    return jnp.broadcast_to(x[:, lane : lane + 1], x.shape)


def solve_kernel(sum_ref, planes_ref, message_ref, work):
    half = LANES
    feat = sum_ref.shape[1]
    top = half + CLASSES
    square = sum_ref[0:half, 0:half]
    turned = square.T
    row, col = iota((half, half), 0), iota((half, half), 1)
    diag = sum_ref[top : top + 1, half:feat]
    first = jnp.where(row >= col, square, turned)
    last = jnp.where(row < col, square, jnp.where(row == col, diag, turned))
    cross = sum_ref[0:half, half:feat]
    sums = sum_ref[half:top, :]
    count_row = sum_ref[top : top + 1, 0:CLASSES]
    eye = iota((CLASSES, CLASSES), 0) == iota((CLASSES, CLASSES), 1)
    counts = jnp.sum(jnp.where(eye, count_row, 0.0), axis=1, keepdims=True)
    total = jnp.sum(counts, axis=0, keepdims=True)
    centers = jnp.sum(sums, axis=0, keepdims=True) / total
    scaled = sums / jnp.maximum(counts, 1.0)
    between = lax.dot_general(
        scaled, sums, TN, precision=HIGHEST, preferred_element_type=jnp.float32
    )
    ridge = jnp.where(row == col, RIDGE, 0.0)
    work[0:half, 0:half] = (first - between[:half, :half]) / total + ridge
    work[0:half, half:feat] = (cross - between[:half, half:]) / total
    work[half:feat, 0:half] = (cross.T - between[half:, :half]) / total
    work[half:feat, half:feat] = (last - between[half:, half:]) / total + ridge
    work[feat : feat + CLASSES, :] = (sums - counts * centers) / total

    rows = feat + CLASSES
    lanes = iota((1, LANES), 1)

    def four(group, base, lane, tile, start):
        pivots = work[pl.ds(group, 8), tile * LANES : (tile + 1) * LANES]
        other = work[pl.ds(group, 8), (1 - tile) * LANES : (2 - tile) * LANES]
        spread = [lane_of(pivots, lane + u) for u in range(4)]
        d = [[spread[u][base + t : base + t + 1, :] for u in range(4)] for t in range(4)]
        a, b, c = d[0][0], d[0][1], d[1][1]
        inv = 1.0 / (a * c - b * b)
        p00, p01, p11 = c * inv, -b * inv, a * inv
        q00, q01, q10, q11 = d[0][2], d[0][3], d[1][2], d[1][3]
        t00, t01 = p00 * q00 + p01 * q10, p00 * q01 + p01 * q11
        t10, t11 = p01 * q00 + p11 * q10, p01 * q01 + p11 * q11
        s00 = d[2][2] - (q00 * t00 + q10 * t10)
        s01 = d[2][3] - (q00 * t01 + q10 * t11)
        s11 = d[3][3] - (q01 * t01 + q11 * t11)
        inv = 1.0 / (s00 * s11 - s01 * s01)
        h00, h01, h11 = s11 * inv, -s01 * inv, s00 * inv
        u00, u01 = t00 * h00 + t01 * h01, t00 * h01 + t01 * h11
        u10, u11 = t10 * h00 + t11 * h01, t10 * h01 + t11 * h11
        e00 = p00 + u00 * t00 + u01 * t01
        e01 = p01 + u00 * t10 + u01 * t11
        e11 = p11 + u10 * t10 + u11 * t11
        dinv = [
            [e00, e01, -u00, -u01],
            [e01, e11, -u10, -u11],
            [-u00, -u10, h00, h01],
            [-u01, -u11, h01, h11],
        ]
        inside = (lanes >= lane) & (lanes < lane + 4)
        near = [
            jnp.where(inside, jnp.where(lanes == lane + t, -1.0, 0.0), pivots[base + t : base + t + 1, :])
            for t in range(4)
        ]
        far = [other[base + t : base + t + 1, :] for t in range(4)]
        mix = lambda r, t: (dinv[t][0] * r[0] + dinv[t][1] * r[1]) + (dinv[t][2] * r[2] + dinv[t][3] * r[3])
        wn = [jnp.broadcast_to(mix(near, t), (8, LANES)) for t in range(4)]
        wf = [jnp.broadcast_to(mix(far, t), (8, LANES)) for t in range(4)]
        inside8 = jnp.broadcast_to(inside, (8, LANES))
        for g in range(start, rows, 8):
            x = work[g : g + 8, tile * LANES : (tile + 1) * LANES]
            y = work[g : g + 8, (1 - tile) * LANES : (2 - tile) * LANES]
            k = [lane_of(x, lane + u) for u in range(4)]
            x = jnp.where(inside8, 0.0, x)
            x = x - ((k[0] * wn[0] + k[1] * wn[1]) + (k[2] * wn[2] + k[3] * wn[3]))
            y = y - ((k[0] * wf[0] + k[1] * wf[1]) + (k[2] * wf[2] + k[3] * wf[3]))
            work[g : g + 8, tile * LANES : (tile + 1) * LANES] = x
            work[g : g + 8, (1 - tile) * LANES : (2 - tile) * LANES] = y

    for pivot in range(0, feat, 4):
        group, base = pivot // 8 * 8, pivot % 8
        four(group, base, pivot % LANES, pivot // LANES, group if base == 0 else group + 8)

    planes = work[feat : feat + CLASSES, :]
    planes_ref[...] = planes
    offsets = -jnp.sum(planes * centers, axis=1, keepdims=True)
    high = offsets.astype(jnp.bfloat16).astype(jnp.float32)
    middle = (offsets - high).astype(jnp.bfloat16).astype(jnp.float32)
    low = offsets - high - middle
    lane = iota((CLASSES, feat), 1)
    coded = jnp.where(lane < LANES, high, jnp.where(lane < LANES + LANES // 2, middle, low))
    message_ref[0:CLASSES, :] = planes.astype(jnp.bfloat16)
    message_ref[CLASSES : 2 * CLASSES, :] = coded.astype(jnp.bfloat16)


def gather_kernel(
    n, sum_ref, planes_ref, out_ref, work, mine_ref, local_sem, send_sems, recv_sems, on_sems, got_sems
):
    me = lax.axis_index("rows")
    near = partner_of(me, 0)
    barrier = pltpu.get_barrier_semaphore()
    for t in range(1, n // 2):
        pl.semaphore_signal(barrier, inc=1, device_id={"rows": lax.rem(me + 2 * t, n)})
    pl.semaphore_signal(barrier, inc=1, device_id={"rows": near})
    solve_kernel(sum_ref, planes_ref, mine_ref, work)
    own = pltpu.make_async_copy(mine_ref, out_ref.at[me], local_sem)
    own.start()
    pl.semaphore_wait(barrier, n // 2)

    def far_copy(t):
        return pltpu.make_async_remote_copy(
            src_ref=mine_ref,
            dst_ref=out_ref.at[me],
            send_sem=send_sems.at[t],
            recv_sem=recv_sems.at[t],
            device_id={"rows": lax.rem(me + 2 * t, n)},
        )

    def near_copy(t):
        source = lax.rem(me + n - 2 * t, n)
        return pltpu.make_async_remote_copy(
            src_ref=mine_ref if t == 0 else out_ref.at[source],
            dst_ref=out_ref.at[source],
            send_sem=on_sems.at[t],
            recv_sem=got_sems.at[t],
            device_id={"rows": near},
        )

    turns = sorted(range(1, n // 2), key=lambda t: -min(t, n // 2 - t))
    for t in turns:
        far_copy(t).start()
    near_copy(0).start()
    own.wait()
    for t in reversed(turns):
        far_copy(t).wait_recv()
        near_copy(t).start()
    for t in turns:
        far_copy(t).wait_send()
    for t in range(n // 2):
        near_copy(t).wait()


def score_kernel(n, owners_ref, x_ref, ids_ref, message_ref, out_ref):
    seg = x_ref.shape[0] * pl.num_programs(0) // n
    some = x_ref.shape[0] // seg
    pieces = seg // LANES
    quarter = LANES + LANES // 2
    for k in range(some):
        node = pl.program_id(0) * some + k
        block = owners_ref[node]
        planes = message_ref[block, 0:CLASSES, :]
        coded = message_ref[block, CLASSES : 2 * CLASSES, :].astype(jnp.float32)
        offsets = coded[:, 0:1] + coded[:, LANES : LANES + 1] + coded[:, quarter : quarter + 1]
        rows = x_ref[k * seg : (k + 1) * seg, :]
        scores = lax.dot_general(planes, rows, NT, preferred_element_type=jnp.float32)
        scores = scores + offsets
        ids = ids_ref[pl.ds(node * pieces, pieces), :]
        for q in range(pieces):
            part = scores[:, q * LANES : (q + 1) * LANES]
            at = k * seg + q * LANES
            out_ref[:, at : at + LANES] = jnp.where(ids[q : q + 1, :] == node, part, 0.0)


def on_device(features, node_ids, labels, owners):
    row_count, feat = features.shape
    n = owners.shape[0]
    seg = row_count // n
    half = feat // 2
    depth = half + CLASSES + 8
    ids = node_ids.reshape(row_count // LANES, LANES)
    tags = labels.reshape(row_count // LANES, LANES)

    whole = pl.BlockSpec(memory_space=pltpu.VMEM)
    summed = pl.pallas_call(
        functools.partial(reduce_kernel, n),
        out_shape=jax.ShapeDtypeStruct((depth, feat), jnp.float32),
        in_specs=[pl.BlockSpec(memory_space=pltpu.HBM)] * 4,
        out_specs=whole,
        scratch_shapes=[
            pltpu.SMEM((n,), jnp.int32),
            pltpu.VMEM((n, seg, feat), features.dtype),
            pltpu.VMEM(ids.shape, jnp.int32),
            pltpu.VMEM(ids.shape, jnp.int32),
            pltpu.VMEM((n, depth, feat), jnp.float32),
            pltpu.VMEM((n, depth, feat), jnp.float32),
            pltpu.SemaphoreType.DMA((4,)),
            pltpu.SemaphoreType.DMA((n,)),
            pltpu.SemaphoreType.DMA((n,)),
        ],
        compiler_params=pltpu.CompilerParams(
            collective_id=0, has_side_effects=True, vmem_limit_bytes=63 << 20
        ),
        name="halving",
    )(owners, features.reshape(n, seg, feat), ids, tags)

    planes, messages = pl.pallas_call(
        functools.partial(gather_kernel, n),
        out_shape=(
            jax.ShapeDtypeStruct((CLASSES, feat), jnp.float32),
            jax.ShapeDtypeStruct((n, 2 * CLASSES, feat), jnp.bfloat16),
        ),
        in_specs=[whole],
        out_specs=(whole, whole),
        scratch_shapes=[
            pltpu.VMEM((feat + CLASSES, feat), jnp.float32),
            pltpu.VMEM((2 * CLASSES, feat), jnp.bfloat16),
            pltpu.SemaphoreType.DMA,
            pltpu.SemaphoreType.DMA((n // 2,)),
            pltpu.SemaphoreType.DMA((n // 2,)),
            pltpu.SemaphoreType.DMA((n // 2,)),
            pltpu.SemaphoreType.DMA((n // 2,)),
        ],
        compiler_params=pltpu.CompilerParams(collective_id=1, has_side_effects=True),
        name="spread",
    )(summed)

    some = 4
    scores = pl.pallas_call(
        functools.partial(score_kernel, n),
        grid_spec=pltpu.PrefetchScalarGridSpec(
            num_scalar_prefetch=1,
            grid=(n // some,),
            in_specs=[
                pl.BlockSpec((some * seg, feat), lambda i, owners: (i, 0)),
                whole,
                whole,
            ],
            out_specs=pl.BlockSpec((CLASSES, some * seg), lambda i, owners: (0, i)),
        ),
        out_shape=jax.ShapeDtypeStruct((CLASSES, row_count), jnp.float32),
        name="scores",
    )(owners, features, ids, messages)
    return planes[None], scores


def solution(mesh):
    in_specs = (P(("leaf", "rows"), None), P(("leaf", "rows")), P(("leaf", "rows")), P("leaf"))
    out_specs = (P(("leaf", "rows"), None, None), P(None, ("leaf", "rows")))
    return jax.shard_map(
        on_device, mesh=mesh, in_specs=in_specs, out_specs=out_specs, check_vma=False
    )
```

profile of v0, /device:TPU:0, one launch (start us, length us, event | category | flops | bytes accessed | tf_op | source)
XLA Modules:
  0.0 52.6 jit_solution(5204127945406509256)
XLA Ops:
  0.6 27.4 %halving.1.sum_ref = f32[152,256]{1,0:T(8,128)} custom-call(s32[16]{0:T(128)} %owners_ref.1, bf16[16,512,256]{2,1,0:T(8,128)(2,1)} %bitcast.4, s32[64,128]{1,0:T(8,128)} %bitcast.5, s32[64,128]{1,0:T(8,128)} %bitcast.7), custom_call_target="tpu_custom_call" | custom-call | tf_op jit(solution)/shard_map/halving/pallas_call | solution.py:351
  28.0 18.4 %spread.1 = (f32[16,256]{1,0:T(8,128)}, bf16[16,32,256]{2,1,0:T(8,128)(2,1)}) custom-call(f32[152,256]{1,0:T(8,128)} %halving.1.sum_ref), custom_call_target="tpu_custom_call" | custom-call | tf_op jit(solution)/shard_map/spread/pallas_call | solution.py:373
  46.5 0.0 copy-start
  46.5 5.5 %scores.1 = f32[16,8192]{1,0:T(8,128)} custom-call(s32[16]{0:T(128)} %owners_ref.1, bf16[8192,256]{1,0:T(8,128)(2,1)} %x_ref.1, s32[64,128]{1,0:T(8,128)} %bitcast.6, bf16[16,32,256]{2,1,0:T(8,128)(2,1)} %get-tuple-element.5.message_ref), custom_call_target="tpu_custom_call" | custom-call | tf_op jit(solution)/shard_map/scores/pallas_call | solution.py:395
  52.0 0.0 copy-done
  52.0 0.6 %copy.7 = f32[1,16,256]{2,1,0:T(8,128)} copy(f32[1,16,256]{2,1,0:T(8,128)S(1)} %bitcast.8) | data formatting | bytes 32768
Async XLA Ops:
  46.5 5.5 %copy-start = (f32[16,256]{1,0:T(8,128)S(1)}, f32[16,256]{1,0:T(8,128)}, u32[]{:S(2)}) copy-start(f32[16,256]{1,0:T(8,128)} %get-tuple-element.4) | copy-start | bytes 49156
where the time goes:
time: 52.9 us; the launch traced here: 52.6 us
  Pallas kernels  51.3 us (97%)
  between operations  0.65 us (1%)
  local copies, waits for them, and re-layouts  0.61 us (1%)
    pallas_call x1, Pallas kernels, on_device(): pl.pallas_call(functools.partial(reduce_kernel, n), out_shape=jax.ShapeDt...  27.4 us
    pallas_call x1, Pallas kernels, on_device(): pl.pallas_call(functools.partial(gather_kernel, n), out_shape=(jax.ShapeD...  18.4 us
    pallas_call x1, Pallas kernels, on_device(): pl.pallas_call(functools.partial(score_kernel, n), grid_spec=pltpu.Prefet...  5.48 us

commit v1 on v0

v1 whole, which is shorter than its diff:
```python
import functools
import jax
import jax.numpy as jnp
from jax import lax
from jax.experimental import pallas as pl
from jax.experimental.pallas import tpu as pltpu
from jax.sharding import PartitionSpec as P

CLASSES = 16
LANES = 128
HALF = LANES // 2
GROUP = 8
RIDGE = 0.1
HIGHEST = lax.Precision.HIGHEST
NN = (((1,), (0,)), ((), ()))
TN = (((0,), (0,)), ((), ()))
NT = (((1,), (1,)), ((), ()))
TOP = HALF + 2 * CLASSES
EARLY = TOP + GROUP
LATE = LANES + HALF
SEND_EARLY, SEND_LATE, HOP, STEP = 1.3, 2.3, 2.0, 0.14
FIRST_EARLY, FIRST_LATE = 6.5, 12.0
VMEM = 67043328


def iota(shape, dim):
    return lax.broadcasted_iota(jnp.int32, shape, dim)


def partner_of(me, bit):
    width = 1 << bit
    return me + width * (1 - 2 * ((me // width) % 2))


def device_at(me, r):
    bit = 0
    while r >> bit:
        if (r >> bit) % 2:
            me = partner_of(me, bit)
        bit += 1
    return me


def exact(a, b, dims):
    return lax.dot_general(a, b, dims, precision=HIGHEST, preferred_element_type=jnp.float32)


def pack(square):
    top, low = square[:HALF, :], square[HALF:, :]
    turned = pltpu.roll(low, HALF, 1)
    row, col = iota((HALF, LANES), 0), iota((HALF, LANES), 1)
    packed = jnp.where((row >= col) | (col >= HALF), top, turned)
    diag = jnp.sum(jnp.where(row + HALF == col, low, 0.0), axis=0, keepdims=True)
    return packed, diag


def unpack(packed, diag):
    row, col = iota((HALF, LANES), 0), iota((HALF, LANES), 1)
    turned = jnp.concatenate([packed, jnp.zeros_like(packed)], axis=0).T
    top = jnp.where((row >= col) | (col >= HALF), packed, turned[:HALF, :])
    last = jnp.where(row < col, packed, jnp.where(row == col, diag, turned[:HALF, :]))
    low = jnp.where(col < HALF, turned[HALF:, :], pltpu.roll(last, HALF, 1))
    return jnp.concatenate([top, low], axis=0)


def one_partial(node, q, x_ref, ids_ref, labels_ref, early, late):
    seg, feat = x_ref.shape[1:]
    pieces = seg // LANES
    ids = ids_ref[pl.ds(node * pieces, pieces), :]
    tags = labels_ref[pl.ds(node * pieces, pieces), :]
    live = ids == node
    length = jnp.sum(live.astype(jnp.float32), axis=(0, 1), keepdims=True)
    x = x_ref[node]
    position = iota((seg, 1), 0).astype(jnp.float32)
    x = jnp.where(position < length, x, jnp.zeros((), x.dtype))
    tags = jnp.where(live, tags, -1)
    hot = jnp.concatenate(
        [tags[k : k + 1, :] == iota((CLASSES, LANES), 0) for k in range(pieces)], axis=1
    )
    hot = hot.astype(jnp.float32).astype(jnp.bfloat16)
    moment = lax.dot_general(x, x, TN, preferred_element_type=jnp.float32)
    sums = jnp.dot(hot, x, preferred_element_type=jnp.float32)
    counts = lax.dot_general(
        jnp.ones((GROUP, seg), jnp.bfloat16), hot, NT, preferred_element_type=jnp.float32
    )
    counts = jnp.concatenate([counts, jnp.zeros((GROUP, LANES - CLASSES), jnp.float32)], axis=1)
    packed, diag = pack(moment[:LANES, :LANES])
    early[q, 0:HALF, :] = packed
    early[q, HALF : HALF + CLASSES, :] = sums[:, :LANES]
    early[q, HALF + CLASSES : TOP, :] = sums[:, LANES:]
    packed, other = pack(moment[LANES:, LANES:])
    diag = diag + pltpu.roll(jnp.broadcast_to(other, (GROUP, LANES)), HALF, 1)
    early[q, TOP:EARLY, :] = jnp.where(iota((GROUP, LANES), 0) == 0, counts, diag)
    late[q, 0:LANES, :] = moment[:LANES, LANES:]
    late[q, LANES:LATE, :] = packed


def lane_of(x, lane):
    return jnp.broadcast_to(x[:, lane : lane + 1], x.shape)


def pivot(rows, at, whole):
    group, base = at // GROUP, at % GROUP
    lanes = iota((1, LANES), 1)
    pivots = rows[group]
    spread = [lane_of(pivots, at + u) for u in range(4)]
    d = [[spread[u][base + t : base + t + 1, :] for u in range(4)] for t in range(4)]
    a, b, c = d[0][0], d[0][1], d[1][1]
    inv = 1.0 / (a * c - b * b)
    p00, p01, p11 = c * inv, -b * inv, a * inv
    q00, q01, q10, q11 = d[0][2], d[0][3], d[1][2], d[1][3]
    t00, t01 = p00 * q00 + p01 * q10, p00 * q01 + p01 * q11
    t10, t11 = p01 * q00 + p11 * q10, p01 * q01 + p11 * q11
    s00 = d[2][2] - (q00 * t00 + q10 * t10)
    s01 = d[2][3] - (q00 * t01 + q10 * t11)
    s11 = d[3][3] - (q01 * t01 + q11 * t11)
    inv = 1.0 / (s00 * s11 - s01 * s01)
    h00, h01, h11 = s11 * inv, -s01 * inv, s00 * inv
    u00, u01 = t00 * h00 + t01 * h01, t00 * h01 + t01 * h11
    u10, u11 = t10 * h00 + t11 * h01, t10 * h01 + t11 * h11
    e00 = p00 + u00 * t00 + u01 * t01
    e01 = p01 + u00 * t10 + u01 * t11
    e11 = p11 + u10 * t10 + u11 * t11
    dinv = [
        [e00, e01, -u00, -u01],
        [e01, e11, -u10, -u11],
        [-u00, -u10, h00, h01],
        [-u01, -u11, h01, h11],
    ]
    inside = (lanes >= at) & (lanes < at + 4)
    near = [
        jnp.where(inside, jnp.where(lanes == at + t, -1.0, 0.0), pivots[base + t : base + t + 1, :])
        for t in range(4)
    ]
    mix = lambda t: (dinv[t][0] * near[0] + dinv[t][1] * near[1]) + (
        dinv[t][2] * near[2] + dinv[t][3] * near[3]
    )
    w = [jnp.broadcast_to(mix(t), (GROUP, LANES)) for t in range(4)]
    inside = jnp.broadcast_to(inside, (GROUP, LANES))
    depth = iota((GROUP, LANES), 0)
    out = list(rows)
    first = 0 if whole else (group if base == 0 else group + 1)
    for g in range(first, len(rows)):
        x = rows[g]
        k = [lane_of(x, at + u) for u in range(4)]
        gone = inside
        if whole and g == group:
            own = (depth >= base) & (depth < base + 4)
            k = [jnp.where(own, jnp.where(depth == base + u, 1.0, 0.0), k[u]) for u in range(4)]
            gone = inside | own
        x = jnp.where(gone, 0.0, x)
        out[g] = x - ((k[0] * w[0] + k[1] * w[1]) + (k[2] * w[2] + k[3] * w[3]))
    return out


def rows_of(x):
    return [x[g : g + GROUP, :] for g in range(0, x.shape[0], GROUP)]


def tree_kernel(
    n,
    owners_hbm,
    x_hbm,
    ids_hbm,
    labels_hbm,
    planes_ref,
    out_ref,
    owners_ref,
    nodes_ref,
    x_ref,
    ids_ref,
    labels_ref,
    early,
    early_in,
    late,
    late_in,
    mine,
    messages,
    scores,
    load_sems,
    early_send,
    early_recv,
    late_send,
    late_recv,
    far_send,
    far_recv,
    near_send,
    near_recv,
):
    bits = n.bit_length() - 1
    seg, feat = x_ref.shape[1:]
    pieces = seg // LANES
    me = lax.axis_index("rows")
    barrier = pltpu.get_barrier_semaphore()
    pairs = [(owners_hbm, owners_ref), (ids_hbm, ids_ref), (labels_hbm, labels_ref), (x_hbm, x_ref)]
    loads = [pltpu.make_async_copy(a, b, load_sems.at[k]) for k, (a, b) in enumerate(pairs)]
    for load in loads:
        load.start()
    for bit in range(bits):
        pl.semaphore_signal(barrier, inc=1, device_id={"rows": partner_of(me, bit)})
    for load in loads:
        load.wait()
    pl.semaphore_wait(barrier, bits)

    def copy_of(part, step, q):
        held, landed, send, recv = (
            (early, early_in, early_send, early_recv),
            (late, late_in, late_send, late_recv),
        )[part]
        return pltpu.make_async_remote_copy(
            src_ref=held.at[q],
            dst_ref=landed.at[q],
            send_sem=send.at[q],
            recv_sem=recv.at[q],
            device_id={"rows": partner_of(me, step)},
        )

    def partial(q):
        slot = 0
        for b in range(bits):
            mine, theirs = (me // (1 << b)) % 2, (q // (1 << (bits - 1 - b))) % 2
            slot = slot + (1 << b) * ((mine + theirs) % 2)
        node = 0
        for k in range(n):
            node = jnp.where(owners_ref[k] == slot, k, node)
        nodes_ref[q] = node
        one_partial(node, q, x_ref, ids_ref, labels_ref, early, late)

    def finish(part, step, q):
        half = n >> (step + 1)
        copy_of(part, step, q + half).wait_recv()
        held, landed = (early, early_in) if part == 0 else (late, late_in)
        held[q] = held[q] + landed[q + half]

    quarter = n // 4

    def turn(i):
        low = quarter - 1 - i % quarter
        for b in range(bits - 2):
            yield (low // (1 << b)) % 2, bits - 3 - b
        yield 1 - i // quarter, bits - 2

    def block_at(i):
        return sum(bit * (1 << place) for bit, place in turn(i))

    def pair(i, carry):
        q = block_at(i)
        partial(q + n // 2)
        copy_of(0, 0, q + n // 2).start()
        copy_of(1, 0, q + n // 2).start()
        partial(q)

        @pl.when(i >= 1)
        def _():
            before = block_at(i - 1)
            finish(0, 0, before)

            @pl.when(i - 1 < quarter)
            def _():
                copy_of(0, 1, before).start()

            finish(1, 0, before)

        @pl.when(i >= quarter + 1)
        def _():
            copy_of(1, 1, block_at(i - 1 - quarter)).start()

        @pl.when(i >= quarter + 2)
        def _():
            before = block_at(i - 2)
            finish(0, 1, before)

            @pl.when(before >= n // 8)
            def _():
                copy_of(0, 2, before).start()

        return carry

    lax.fori_loop(0, n // 2, pair, 0)
    finish(0, 0, 0)
    copy_of(1, 1, block_at(quarter - 1)).start()
    finish(1, 0, 0)

    def times(first, gap):
        when = {(1, block_at(quarter + j)): first + gap * j for j in range(quarter)}
        for step in range(2, bits):
            half = n >> (step + 1)
            for q in range(half):
                when[step, q] = max(when[step - 1, q], when[step - 1, q + half] + HOP + gap)
        return when

    done = {block_at(i) for i in range(quarter, n // 2 - 2)}
    first = times(FIRST_EARLY, SEND_EARLY)
    last = times(FIRST_LATE, SEND_LATE)
    events = [(at, step, 0, q) for (step, q), at in first.items() if step > 1 or q not in done]
    events = sorted(events + [(at, step, 1, q) for (step, q), at in last.items()])
    begin = first[bits - 1, 0]

    def advance(part, step, q):
        finish(part, step, q)
        if step < bits - 1 and q >= n >> (step + 2):
            copy_of(part, step + 1, q).start()

    while events and events[0][0] <= begin:
        at, step, part, q = events.pop(0)
        advance(part, step, q)

    sums = jnp.concatenate(
        [early[0, HALF : HALF + CLASSES, :], early[0, HALF + CLASSES : TOP, :]], axis=1
    )
    count_row = early[0, TOP : TOP + 1, 0:CLASSES]
    eye = iota((CLASSES, CLASSES), 0) == iota((CLASSES, CLASSES), 1)
    counts = jnp.sum(jnp.where(eye, count_row, 0.0), axis=1, keepdims=True)
    total = jnp.sum(counts, axis=0, keepdims=True)
    centers = jnp.sum(sums, axis=0, keepdims=True) / total
    scaled = sums / jnp.maximum(counts, 1.0)
    row, col = iota((LANES, LANES), 0), iota((LANES, LANES), 1)
    ridge = jnp.where(row == col, RIDGE, 0.0)
    diag = early[0, TOP + 1 : TOP + 2, :]
    between = exact(scaled, sums, TN)
    shifts = (sums - counts * centers) / total
    square = unpack(early[0, 0:HALF, :], pltpu.roll(jnp.broadcast_to(diag, (GROUP, LANES)), HALF, 1)[0:1, :])
    rows = rows_of((square - between[:LANES, :LANES]) / total + ridge)
    for turned in range(LANES // 4):
        while events and events[0][0] <= begin + STEP * turned:
            at, step, part, q = events.pop(0)
            advance(part, step, q)
        rows = pivot(rows, 4 * turned, True)
    for at, step, part, q in events:
        advance(part, step, q)

    inverse = jnp.concatenate(rows, axis=0)
    cross = (late[0, 0:LANES, :] - between[:LANES, LANES:]) / total
    square = unpack(late[0, LANES:LATE, :], diag)
    last = (square - between[LANES:, LANES:]) / total + ridge
    gain = exact(inverse, cross, NN)
    schur = last - exact(cross, gain, TN)
    right = shifts[:, LANES:] - exact(shifts[:, :LANES], gain, NN)
    left = exact(shifts[:, :LANES], inverse, NN)
    rows = rows_of(schur) + rows_of(right)
    for step in range(LANES // 4):
        rows = pivot(rows, 4 * step, False)
    right = jnp.concatenate(rows[LANES // GROUP :], axis=0)
    left = left - exact(right, gain, NT)
    planes = jnp.concatenate([left, right], axis=1)
    planes_ref[...] = planes
    offsets = -jnp.sum(planes * centers, axis=1, keepdims=True)
    high = offsets.astype(jnp.bfloat16).astype(jnp.float32)
    middle = (offsets - high).astype(jnp.bfloat16).astype(jnp.float32)
    low = offsets - high - middle
    lane = iota((CLASSES, LANES), 1)
    third = LANES // 4
    coded = jnp.where(lane < third, high, jnp.where(lane < 2 * third, middle, low))
    mine[:, 0:feat] = planes.astype(jnp.bfloat16)
    mine[:, feat : feat + LANES] = coded.astype(jnp.bfloat16)

    def far_copy(r):
        return pltpu.make_async_remote_copy(
            src_ref=mine,
            dst_ref=messages.at[r],
            send_sem=far_send.at[r // 2],
            recv_sem=far_recv.at[r // 2],
            device_id={"rows": device_at(me, r)},
        )

    def near_copy(r):
        return pltpu.make_async_remote_copy(
            src_ref=mine if r == 0 else messages.at[r],
            dst_ref=messages.at[r + 1],
            send_sem=near_send.at[r // 2],
            recv_sem=near_recv.at[r // 2],
            device_id={"rows": partner_of(me, 0)},
        )

    def score(r):
        q = sum(((r >> b) % 2) << (bits - 1 - b) for b in range(bits))
        node = nodes_ref[q]
        message = mine if r == 0 else messages.at[r]
        coded = message[:, feat : feat + LANES].astype(jnp.float32)
        offsets = coded[:, 0:1] + coded[:, third : third + 1] + coded[:, 2 * third : 2 * third + 1]
        values = lax.dot_general(
            message[:, 0:feat], x_ref[node], NT, preferred_element_type=jnp.float32
        )
        values = values + offsets
        ids = ids_ref[pl.ds(node * pieces, pieces), :]
        for k in range(pieces):
            part = values[:, k * LANES : (k + 1) * LANES]
            scores[r, :, k * LANES : (k + 1) * LANES] = jnp.where(ids[k : k + 1, :] == node, part, 0.0)

    turns = list(range(2, n, 2))
    for r in reversed(turns):
        far_copy(r).start()
    near_copy(0).start()
    score(0)
    for r in turns:
        far_copy(r).wait_recv()
        near_copy(r).start()
        near_copy(r - 2).wait_recv()
        score(r - 1)
        score(r)
    near_copy(n - 2).wait_recv()
    score(n - 1)
    for k in range(n):
        out_ref[:, k * seg : (k + 1) * seg] = scores[lax.bitwise_xor(owners_ref[k], me)]
    for part, send in ((0, early_send), (1, late_send)):
        for step in range(bits):
            half = n >> (step + 1)
            for q in range(half, 2 * half):
                copy_of(part, step, q).wait_send()
    for r in turns:
        far_copy(r).wait_send()
    for r in range(0, n, 2):
        near_copy(r).wait_send()


def on_device(features, node_ids, labels, owners):
    row_count, feat = features.shape
    n = owners.shape[0]
    seg = row_count // n
    ids = node_ids.reshape(row_count // LANES, LANES)
    tags = labels.reshape(row_count // LANES, LANES)
    hbm = pl.BlockSpec(memory_space=pltpu.HBM)
    whole = pl.BlockSpec(memory_space=pltpu.VMEM)
    dma = pltpu.SemaphoreType.DMA

    planes, scores = pl.pallas_call(
        functools.partial(tree_kernel, n),
        out_shape=(
            pltpu.VMEM((CLASSES, feat), jnp.float32),
            pltpu.VMEM((CLASSES, row_count), jnp.float32),
        ),
        in_specs=[hbm] * 4,
        out_specs=(whole, whole),
        scratch_shapes=[
            pltpu.SMEM((n,), jnp.int32),
            pltpu.SMEM((n,), jnp.int32),
            pltpu.VMEM((n, seg, feat), features.dtype),
            pltpu.VMEM(ids.shape, jnp.int32),
            pltpu.VMEM(ids.shape, jnp.int32),
            pltpu.VMEM((n, EARLY, LANES), jnp.float32),
            pltpu.VMEM((n, EARLY, LANES), jnp.float32),
            pltpu.VMEM((n, LATE, LANES), jnp.float32),
            pltpu.VMEM((n, LATE, LANES), jnp.float32),
            pltpu.VMEM((CLASSES, feat + LANES), jnp.bfloat16),
            pltpu.VMEM((n, CLASSES, feat + LANES), jnp.bfloat16),
            pltpu.VMEM((n, CLASSES, seg), jnp.float32),
            dma((4,)),
            dma((n,)),
            dma((n,)),
            dma((n,)),
            dma((n,)),
            dma((n // 2,)),
            dma((n // 2,)),
            dma((n // 2,)),
            dma((n // 2,)),
        ],
        compiler_params=pltpu.CompilerParams(
            collective_id=0, has_side_effects=True, vmem_limit_bytes=VMEM - 4 * CLASSES * (row_count + feat)
        ),
        name="tree",
    )(owners, features.reshape(n, seg, feat), ids, tags)

    return planes[None], scores


def solution(mesh):
    in_specs = (P(("leaf", "rows"), None), P(("leaf", "rows")), P(("leaf", "rows")), P("leaf"))
    out_specs = (P(("leaf", "rows"), None, None), P(None, ("leaf", "rows")))
    return jax.shard_map(
        on_device, mesh=mesh, in_specs=in_specs, out_specs=out_specs, check_vma=False
    )
```

time: 52.9 us -> 47.3 us (0.89)
  Pallas kernels: 51.3 us -> 45.2 us
  local copies, waits for them, and re-layouts: 0.61 us -> 1.4 us
    pallas_call x3 -> x1, Pallas kernels: 51.3 us -> 45.2 us  [on_device(): pl.pallas_call(functools.partial(tree_kernel, n), out_shape=(pltpu.VMEM((...]
    unnamed x3 -> x2, local copies, waits for them, and re-layouts: 0.61 us -> 1.4 us
where the time goes in v1:
time: 47.3 us; the launch traced here: 47.2 us
  Pallas kernels  45.2 us (96%)
  local copies, waits for them, and re-layouts  1.4 us (3%)
  between operations  0.64 us (1%)
    pallas_call x1, Pallas kernels, on_device(): pl.pallas_call(functools.partial(tree_kernel, n), out_shape=(pltpu.VMEM((...  45.2 us
    unnamed x2, local copies, waits for them, and re-layouts  1.4 us

profile of v1, /device:TPU:0, one launch (start us, length us, event | category | flops | bytes accessed | tf_op | source)
XLA Modules:
  0.0 47.2 jit_solution(6849197309484979310)
XLA Ops:
  0.6 45.2 %tree.1 = (f32[16,256]{1,0:T(8,128)S(1)}, f32[16,8192]{1,0:T(8,128)S(1)}) custom-call(s32[16]{0:T(128)} %owners_hbm.1, bf16[16,512,256]{2,1,0:T(8,128)(2,1)} %bitcast.5, s32[64,128]{1,0:T(8,128)} %bitcast.6, s32[64,128]{1,0:T(8,128)} %bitcast.7), custom_call_target="tpu_custom_call" | custom-call | tf_op jit(solution)/shard_map/tree/pallas_call | solution.py:426
  45.8 0.6 %copy.8 = f32[1,16,256]{2,1,0:T(8,128)} copy(f32[1,16,256]{2,1,0:T(8,128)S(1)} %bitcast.4) | data formatting | bytes 32768
  46.4 0.8 %copy.9 = f32[16,8192]{1,0:T(8,128)} copy(f32[16,8192]{1,0:T(8,128)S(1)} %get-tuple-element.7) | data formatting | bytes 1048576
